TPU v7x, 32 devices: a whole 2x2x4 slice. The times are simulated.
32 devices in a mesh: dp: 8 (over z, x), ctx: 4 (over y, core).
Axes of the slice: x: 2, y: 2, z: 4, core: 2. Of those that a mesh axis runs over, the one named last changes fastest.
Arguments:
- tokens: bfloat16 [64, 1024, 576], P('dp', 'ctx'), may hold values from -6 to 6
- w_qkv: bfloat16 [552960], P(('dp', 'ctx')), may hold values from -0.25 to 0.25
- w_out: bfloat16 [331776], P(('dp', 'ctx')), may hold values from -1 to 1
- w_gate_up: bfloat16 [1769472], P(('dp', 'ctx')), may hold values from -0.25 to 0.25
- w_down: bfloat16 [884736], P(('dp', 'ctx')), may hold values from -0.15625 to 0.15625
- gains: bfloat16 [1152], P(('dp', 'ctx')), may hold values from 0.099609375 to 1.8984375
- cotangent: bfloat16 [64, 1024, 576], P('dp', 'ctx'), may hold values from -6 to 6
Outputs:
- output: bfloat16 [64, 1024, 576], P('dp', 'ctx')
- grad_input: bfloat16 [64, 1024, 576], P('dp', 'ctx')
- grad_qkv: float32 [552960], P(('dp', 'ctx'))
- grad_out: float32 [331776], P(('dp', 'ctx'))
- grad_gate_up: float32 [1769472], P(('dp', 'ctx'))
- grad_down: float32 [884736], P(('dp', 'ctx'))
- grad_gains: float32 [1152], P(('dp', 'ctx'))
All inputs are finite; a program needn't handle non-finite values.
Results may differ from a plain program's by a relative error of at most 0.014.
Values may be sent and summed in bfloat16 or wider, within the bound.
No kernel may reach another device: no remote copies, remote signals or barrier semaphores. Data moves between devices by JAX's collectives and lax.ppermute only.
A program may use at most 384 MiB of HBM per device.

v0:
```python
import math
import jax
import jax.numpy as jnp
from jax import lax
from jax.sharding import PartitionSpec as P

D = 576
HEADS = 9
KV_HEADS = 3
HEAD = 64
FF = 1536
QKVW = 960
EPSILON = 1e-05
THETA_BASE = 100000.0
NEG_FILL = -1e30


def angle_tables(positions, width):
    halves = jnp.arange(0, width, 2).astype(jnp.float32) / width
    inverse = jnp.exp(-math.log(THETA_BASE) * halves)
    angles = positions.astype(jnp.float32)[:, None] * inverse[None, :]
    angles = jnp.concatenate([angles, angles], axis=-1)
    return (jnp.cos(angles), jnp.sin(angles))


def rotate(values, cosine, sine):
    half = values.shape[-1] // 2
    turned = jnp.concatenate([-values[..., half:], values[..., :half]], axis=-1)
    return values * cosine + turned * sine


def unrotate(grads, cosine, sine):
    half = grads.shape[-1] // 2
    scaled = grads * sine
    turned = jnp.concatenate([scaled[..., half:], -scaled[..., :half]], axis=-1)
    return grads * cosine + turned


def fetch(part_qkv, part_out, part_gu, part_down, part_gains):
    result = (
        lax.all_gather(part_qkv, ("dp", "ctx"), axis=0, tiled=True),
        lax.all_gather(part_out, ("dp", "ctx"), axis=0, tiled=True),
        lax.all_gather(part_gu, ("dp", "ctx"), axis=0, tiled=True),
        lax.all_gather(part_down, ("dp", "ctx"), axis=0, tiled=True),
        lax.all_gather(part_gains, ("dp", "ctx"), axis=0, tiled=True),
    )
    return result


def settle(term_qkv, term_out, term_gu, term_down, term_gains):
    result = (
        lax.psum_scatter(term_qkv, ("dp", "ctx"), scatter_dimension=0, tiled=True),
        lax.psum_scatter(term_out, ("dp", "ctx"), scatter_dimension=0, tiled=True),
        lax.psum_scatter(term_gu, ("dp", "ctx"), scatter_dimension=0, tiled=True),
        lax.psum_scatter(term_down, ("dp", "ctx"), scatter_dimension=0, tiled=True),
        lax.psum_scatter(term_gains, ("dp", "ctx"), scatter_dimension=0, tiled=True),
    )
    return result


def attention_scores(queries, keys, allowed):
    raw = jnp.einsum("sqhgd,skhd->shgqk", queries, keys, preferred_element_type=jnp.float32) * 0.125
    return jnp.where(allowed, raw, NEG_FILL)


def local(tokens, w_qkv, w_out, w_gate_up, w_down, gains, cotangent):
    seqs_here = tokens.shape[0]
    span = tokens.shape[1]
    group = HEADS // KV_HEADS
    kv_width = KV_HEADS * HEAD
    row_count = seqs_here * span
    first = fetch(w_qkv, w_out, w_gate_up, w_down, gains)
    mat_qkv = first[0].reshape(D, QKVW)
    mat_out = first[1].reshape(D, D)
    mat_gu = first[2].reshape(D, 2 * FF)
    mat_down = first[3].reshape(FF, D)
    gain_one = first[4][:D].astype(jnp.float32)
    gain_two = first[4][D:].astype(jnp.float32)
    rows = tokens.reshape(row_count, D).astype(jnp.float32)
    inverse_one = lax.rsqrt(jnp.mean(rows * rows, axis=-1, keepdims=True) + EPSILON)
    normal_one = rows * inverse_one
    normed_one = (normal_one * gain_one).astype(jnp.bfloat16)
    projected = jnp.dot(normed_one, mat_qkv, preferred_element_type=jnp.float32)
    here = lax.axis_index("ctx") * span + jnp.arange(span)
    cos_here, sin_here = angle_tables(here, HEAD)
    cos_q = cos_here[None, :, None, :]
    sin_q = sin_here[None, :, None, :]
    queries = rotate(projected[:, :D].reshape(seqs_here, span, HEADS, HEAD), cos_q, sin_q)
    query_low = queries.astype(jnp.bfloat16).reshape(seqs_here, span, KV_HEADS, group, HEAD)
    key_low = rotate(
        projected[:, D : D + kv_width].reshape(seqs_here, span, KV_HEADS, HEAD), cos_q, sin_q
    ).astype(jnp.bfloat16)
    value_low = projected[:, D + kv_width :].astype(jnp.bfloat16)
    stacked = jnp.concatenate(
        [key_low.reshape(seqs_here, span, kv_width), value_low.reshape(seqs_here, span, kv_width)],
        axis=-1,
    )
    gathered = lax.all_gather(stacked, "ctx", axis=1, tiled=True)
    total_len = gathered.shape[1]
    key_all = gathered[..., :kv_width].reshape(seqs_here, total_len, KV_HEADS, HEAD)
    value_all = gathered[..., kv_width:].reshape(seqs_here, total_len, KV_HEADS, HEAD)
    places = jnp.arange(total_len)
    allowed = here[:, None] >= places[None, :]
    scores = attention_scores(query_low, key_all, allowed)
    highest = jnp.max(scores, axis=-1, keepdims=True)
    expo = jnp.exp(scores - highest)
    totals = jnp.sum(expo, axis=-1, keepdims=True)
    probs = expo / totals
    log_total = highest + jnp.log(totals)
    prob_low = probs.astype(jnp.bfloat16)
    mixed = jnp.einsum("shgqk,skhd->sqhgd", prob_low, value_all, preferred_element_type=jnp.float32)
    mixed_low = mixed.reshape(row_count, D).astype(jnp.bfloat16)
    residual = rows + jnp.dot(mixed_low, mat_out, preferred_element_type=jnp.float32)
    inverse_two = lax.rsqrt(jnp.mean(residual * residual, axis=-1, keepdims=True) + EPSILON)
    normal_two = residual * inverse_two
    normed_two = (normal_two * gain_two).astype(jnp.bfloat16)
    gate_up = jnp.dot(normed_two, mat_gu, preferred_element_type=jnp.float32)
    gate_part = gate_up[:, :FF]
    up_part = gate_up[:, FF:]
    sigmoid_gate = 1.0 / (1.0 + jnp.exp(-gate_part))
    activated = gate_part * sigmoid_gate
    product_low = (activated * up_part).astype(jnp.bfloat16)
    output = (residual + jnp.dot(product_low, mat_down, preferred_element_type=jnp.float32)).astype(
        jnp.bfloat16
    )
    second = fetch(w_qkv, w_out, w_gate_up, w_down, gains)
    back_qkv = second[0].reshape(D, QKVW)
    back_out = second[1].reshape(D, D)
    back_gu = second[2].reshape(D, 2 * FF)
    back_down = second[3].reshape(FF, D)
    grad_rows = cotangent.reshape(row_count, D)
    grad_down = jnp.dot(product_low.T, grad_rows, preferred_element_type=jnp.float32)
    grad_product = jnp.dot(grad_rows, back_down.T, preferred_element_type=jnp.float32)
    grad_gate = grad_product * up_part * sigmoid_gate * (1.0 + gate_part * (1.0 - sigmoid_gate))
    grad_up = grad_product * activated
    grad_gu_low = jnp.concatenate([grad_gate, grad_up], axis=-1).astype(jnp.bfloat16)
    grad_gate_up = jnp.dot(normed_two.T, grad_gu_low, preferred_element_type=jnp.float32)
    grad_normed_two = jnp.dot(grad_gu_low, back_gu.T, preferred_element_type=jnp.float32)
    grad_gain_two = jnp.sum(grad_normed_two * normal_two, axis=0)
    scaled_two = grad_normed_two * gain_two
    grad_residual = grad_rows.astype(jnp.float32) + inverse_two * (
        scaled_two - normal_two * jnp.mean(scaled_two * normal_two, axis=-1, keepdims=True)
    )
    grad_branch_low = grad_residual.astype(jnp.bfloat16)
    grad_out = jnp.dot(mixed_low.T, grad_branch_low, preferred_element_type=jnp.float32)
    grad_mixed_low = jnp.dot(
        grad_branch_low, back_out.T, preferred_element_type=jnp.float32
    ).astype(jnp.bfloat16)
    grad_mixed_low = grad_mixed_low.reshape(seqs_here, span, KV_HEADS, group, HEAD)
    scores_again = attention_scores(query_low, key_all, allowed)
    probs_again = jnp.exp(scores_again - log_total)
    prob_again_low = probs_again.astype(jnp.bfloat16)
    grad_probs = jnp.einsum(
        "sqhgd,skhd->shgqk", grad_mixed_low, value_all, preferred_element_type=jnp.float32
    )
    centre = jnp.sum(probs_again * grad_probs, axis=-1, keepdims=True)
    grad_scores_low = (probs_again * (grad_probs - centre)).astype(jnp.bfloat16)
    grad_queries = 0.125 * jnp.einsum(
        "shgqk,skhd->sqhgd", grad_scores_low, key_all, preferred_element_type=jnp.float32
    )
    grad_keys = 0.125 * jnp.einsum(
        "shgqk,sqhgd->skhd", grad_scores_low, query_low, preferred_element_type=jnp.float32
    )
    grad_values = jnp.einsum(
        "shgqk,sqhgd->skhd", prob_again_low, grad_mixed_low, preferred_element_type=jnp.float32
    )
    cos_all, sin_all = angle_tables(places, HEAD)
    grad_queries = unrotate(grad_queries.reshape(seqs_here, span, HEADS, HEAD), cos_q, sin_q)
    grad_keys = unrotate(grad_keys, cos_all[None, :, None, :], sin_all[None, :, None, :])
    kv_terms = jnp.concatenate(
        [
            grad_keys.reshape(seqs_here, total_len, kv_width),
            grad_values.reshape(seqs_here, total_len, kv_width),
        ],
        axis=-1,
    ).astype(jnp.bfloat16)
    kv_owned = lax.psum_scatter(kv_terms, "ctx", scatter_dimension=1, tiled=True).astype(
        jnp.float32
    )
    grad_proj_low = jnp.concatenate(
        [grad_queries.reshape(row_count, D), kv_owned.reshape(row_count, 2 * kv_width)], axis=-1
    ).astype(jnp.bfloat16)
    grad_qkv = jnp.dot(normed_one.T, grad_proj_low, preferred_element_type=jnp.float32)
    grad_normed_one = jnp.dot(grad_proj_low, back_qkv.T, preferred_element_type=jnp.float32)
    grad_gain_one = jnp.sum(grad_normed_one * normal_one, axis=0)
    scaled_one = grad_normed_one * gain_one
    grad_input = grad_residual + inverse_one * (
        scaled_one - normal_one * jnp.mean(scaled_one * normal_one, axis=-1, keepdims=True)
    )
    owned = settle(
        grad_qkv.reshape(-1),
        grad_out.reshape(-1),
        grad_gate_up.reshape(-1),
        grad_down.reshape(-1),
        jnp.concatenate([grad_gain_one, grad_gain_two]),
    )
    return (
        output.reshape(tokens.shape),
        grad_input.astype(jnp.bfloat16).reshape(tokens.shape),
        owned[0],
        owned[1],
        owned[2],
        owned[3],
        owned[4],
    )


def solution(mesh):
    in_specs = (
        P("dp", "ctx", None),
        P(("dp", "ctx")),
        P(("dp", "ctx")),
        P(("dp", "ctx")),
        P(("dp", "ctx")),
        P(("dp", "ctx")),
        P("dp", "ctx", None),
    )
    out_specs = (
        P("dp", "ctx", None),
        P("dp", "ctx", None),
        P(("dp", "ctx")),
        P(("dp", "ctx")),
        P(("dp", "ctx")),
        P(("dp", "ctx")),
        P(("dp", "ctx")),
    )
    return jax.shard_map(local, mesh=mesh, in_specs=in_specs, out_specs=out_specs, check_vma=False)
```

profile of v0, /device:TPU:0, one launch (start us, length us, event | category | flops | bytes accessed | tf_op | source)
XLA Modules:
  0.0 946.1 jit_solution(13876361599420750853)
XLA Ops:
  11.1 42.0 %all-reduce = bf16[1152]{0:T(1024)(128)(2,1)S(1)} all-reduce(bf16[1152]{0:T(1024)(128)(2,1)S(1)} %dynamic-update-slice), channel_id=1, replica_groups=mesh['dp'=8,'ctx'=4] {'dp','ctx'}, use_global_device_ids=true, to_apply=%add | all-reduce | flops 1152 | bytes 4608
  59.9 11.1 %all-gather.13.cloned.1.call-done = bf16[32,1,17280]{2,1,0:T(2,128)(2,1)} async-done(((bf16[1,1,17280]{2,1,0:T(2,128)(2,1)}), bf16[32,1,17280]{2,1,0:T(2,128)(2,1)}) %all-gather.13.cloned.1.call-update) | async-done | bytes 1105936 | tf_op jit(solution)/shard_map/all_gather | solution.py:41
  71.0 7.7 reduce.1
  80.8 4.7 fusion.55
  90.7 46.2 %all-gather.1 = bf16[32,1,10368]{2,1,0:T(2,128)(2,1)} all-gather(bf16[1,1,10368]{2,1,0:T(2,128)(2,1)S(1)} %reshape.317), channel_id=1, replica_groups=mesh['dp'=8,'ctx'=4] {'dp','ctx'}, dimensions={0}, use_global_device_ids=true | all-gather | bytes 684288 | tf_op jit(solution)/shard_map/all_gather | solution.py:42
  136.9 5.0 reduce.2
  143.7 3.4 copy.96
  147.5 2.8 copy.94
  161.3 4.7 reshape.298
  165.9 25.6 %all-gather.9.cloned.1.call-done = bf16[1769472]{0:T(1024)(128)(2,1)} async-done(((bf16[55296]{0:T(1024)(128)(2,1)}), bf16[1769472]{0:T(1024)(128)(2,1)}) %all-gather.9.cloned.1.call-update) | async-done | bytes 3538960 | tf_op jit(solution)/shard_map/all_gather | solution.py:43
  191.5 6.9 reshape.297
  198.5 41.1 %all-gather.7.cloned.1.call-done = bf16[8,1024,384]{1,0,2:T(8,128)(2,1)} async-done(((bf16[8,256,384]{1,0,2:T(8,128)(2,1)}), bf16[8,1024,384]{1,0,2:T(8,128)(2,1)}) %all-gather.7.cloned.1.call-update) | async-done | bytes 6291472 | tf_op jit(solution)/shard_map/all_gather | solution.py:98
  239.6 3.6 fusion.53
  244.9 3.5 copy.59
  248.4 27.1 %fusion.9 = (f32[8,3,3,256]{3,2,1,0:T(4,128)S(1)}, f32[8,3,1024,256,3]{3,2,4,1,0:T(8,128)}) fusion(pred[256,1024]{0,1:T(8,128)(4,1)S(1)} %iota_compare_fusion, bf16[8,1024,3,64,1]{1,3,4,2,0:T(8,128)(2,1)S(1)} %bitcast.178, bf16[8,256,3,3,64]{1,4,3,2,0:T(8,128)(2,1)S(1)} %fusion.18), kind=kOutput, calls=%fused_computation.14 | convolution fusion | flops 2472523776 | bytes 81338368 | tf_op jit(solution)/shard_map/sqhgd,skhd->shgqk/dot_general | solution.py:62
  275.5 24.8 %fusion.3 = f32[8,3,3,256]{3,2,1,0:T(4,128)} fusion(f32[8,3,3,256]{3,2,1,0:T(4,128)S(1)} %get-tuple-element.57, f32[8,3,1024,256,3]{3,2,4,1,0:T(8,128)} %get-tuple-element.58, pred[256,1024]{0,1:T(8,128)(4,1)S(1)} %iota_compare_fusion), kind=kLoop, calls=%fused_computation.9 | loop fusion | flops 75479040 | bytes 75907072 | tf_op jit(solution)/shard_map/reduce_sum | solution.py:107
  301.9 29.8 %convert_bitcast_fusion.1 = bf16[8,256,3,3,64]{1,4,3,2,0:T(8,128)(2,1)} fusion(bf16[8,1024,3,64,1]{1,3,4,2,0:T(8,128)(2,1)S(1)} %bitcast.194, f32[8,3,3,256]{3,2,1,0:T(4,128)} %fusion.3, f32[8,3,3,256]{3,2,1,0:T(4,128)S(1)} %get-tuple-element.57, f32[8,3,1024,256,3]{3,2,4,1,0:T(8,128)} %get-tuple-element.58, pred[256,1024]{0,1:T(8,128)(4,1)S(1)} %iota_compare_fusion), kind=kOutput, calls=%fused_computation.67 | convolution fusion | flops 2511470592 | bytes 81412096 | tf_op jit(solution)/shard_map/shgqk,skhd->sqhgd/dot_general | solution.py:111
  331.8 3.2 copy.65
  335.8 5.5 multiply_reduce_fusion.4
  341.3 14.0 %fusion.51 = f32[2048,3072]{1,0:T(8,128)} fusion(bf16[576,3072]{1,0:T(8,128)(2,1)S(1)} %copy-done.15, f32[2048,576]{0,1:T(8,128)S(1)} %get-tuple-element.60, f32[576]{0:T(1024)S(1)} %copy-done.34, f32[2048]{0:T(1024)S(1)} %add_rsqrt_fusion), kind=kOutput, calls=%fused_computation.114 | convolution fusion | flops 7251296256 | bytes 33433856 | tf_op jit(solution)/shard_map/dot_general | solution.py:117
  355.3 21.5 %multiply_convert_fusion.1 = (bf16[2048,1536]{1,0:T(8,128)(2,1)}, bf16[2048,1536]{1,0:T(8,128)(2,1)}, bf16[2048,1536]{1,0:T(8,128)(2,1)}) fusion(f32[2048,3072]{1,0:T(8,128)} %fusion.51, bf16[2048,576]{0,1:T(8,128)(2,1)} %bitcast.197, bf16[1536,576]{1,0:T(8,128)(2,1)} %reshape.298), kind=kOutput, calls=%fused_computation.17 | convolution fusion | flops 3671064576 | bytes 48168960 | tf_op jit(solution)/shard_map/dot_general | solution.py:133
  376.8 13.5 %multiply_reduce_fusion = (f32[576]{0:T(1024)}, f32[2048]{0:T(1024)S(1)}, f32[2048,576]{0,1:T(8,128)S(1)}) fusion(f32[2048,576]{0,1:T(8,128)} %copy-done, f32[2048]{0:T(1024)S(1)} %add_rsqrt_fusion, f32[576]{0:T(1024)S(1)} %copy-done.34, bf16[576,3072]{1,0:T(8,128)(2,1)} %reshape.297, bf16[2048,1536]{1,0:T(8,128)(2,1)} %get-tuple-element.37, ...), kind=kOutput, calls=%fused_computation.41 | convolution fusion | flops 7279998464 | bytes 25580032 | tf_op jit(solution)/shard_map/dot_general | solution.py:138
  396.3 30.7 %bitcast_convert_fusion = bf16[8,3,64,1024]{3,2,1,0:T(8,128)(2,1)} fusion(f32[8,3,3,256]{3,2,1,0:T(4,128)S(1)} %copy-done.26, f32[8,3,1024,256,3]{3,2,4,1,0:T(8,128)} %get-tuple-element.58, pred[256,1024]{0,1:T(8,128)(4,1)S(1)} %iota_compare_fusion, bf16[8,256,3,3,64]{1,0,4,3,2:T(8,128)(2,1)S(1)} %bitcast.203), kind=kOutput, calls=%fused_computation.29 | convolution fusion | flops 2492989440 | bytes 81338368 | tf_op jit(solution)/shard_map/shgqk,sqhgd->skhd/dot_general | solution.py:164
  427.0 57.9 %fusion = (f32[8,3,3,256]{3,2,1,0:T(4,128)}, f32[8,3,1024,256,3]{3,2,4,1,0:T(8,128)}) fusion(f32[8,3,3,256]{3,2,1,0:T(4,128)S(1)} %copy-done.26, f32[8,3,1024,256,3]{3,2,4,1,0:T(8,128)} %get-tuple-element.58, pred[256,1024]{0,1:T(8,128)(4,1)S(1)} %iota_compare_fusion, bf16[8,1024,3,64,1]{1,3,4,2,0:T(8,128)(2,1)S(1)} %bitcast.195, ...), kind=kOutput, calls=%fused_computation.2 | convolution fusion | flops 2510272512 | bytes 156909568 | tf_op jit(solution)/shard_map/sqhgd,skhd->shgqk/dot_general | solution.py:153
  484.9 6.2 copy.77
  491.1 59.9 %fusion.2 = bf16[8,3,3,256,1024]{3,4,2,1,0:T(8,128)(2,1)} fusion(f32[8,3,1024,256,3]{3,2,4,1,0:T(8,128)} %get-tuple-element.63, f32[8,3,3,256]{3,2,1,0:T(4,128)S(1)} %copy-done.27, f32[8,3,3,256]{3,2,1,0:T(4,128)S(1)} %copy-done.26, f32[8,3,1024,256,3]{3,2,4,1,0:T(8,128)} %get-tuple-element.58, pred[256,1024]{0,1:T(8,128)(4,1)S(1)} %iota_compare_fusion), kind=kLoop, calls=%fused_computation.4 | loop fusion | flops 113246208 | bytes 189153280 | tf_op jit(solution)/shard_map/convert_element_type | solution.py:157
  551.0 19.4 %bitcast_multiply_fusion.1 = (f32[8,1024,3,64]{1,3,2,0:T(8,128)S(1)}, f32[8,3,64,1024,1]{3,2,4,1,0:T(8,128)}) fusion(f32[1024,64]{0,1:T(8,128)S(1)} %copy-done.6, bf16[8,256,3,3,64]{1,4,3,2,0:T(8,128)(2,1)} %copy-done.5, bf16[8,3,3,256,1024]{3,4,2,1,0:T(8,128)(2,1)} %fusion.2), kind=kOutput, calls=%fused_computation.30 | convolution fusion | flops 2417491968 | bytes 52953088 | tf_op jit(solution)/shard_map/shgqk,sqhgd->skhd/dot_general | solution.py:161
  572.9 5.5 fusion.13
  578.3 4.1 copy.76
  582.5 8.4 pad_maximum_fusion.3
  592.2 4.4 copy.106
  596.6 8.9 fusion.56
  605.5 5.3 reshape.311
  610.8 13.1 %fusion.19 = f32[72,24,8,128]{3,2,1,0:T(8,128)S(1)} fusion(bf16[2048,1536]{1,0:T(8,128)(2,1)} %get-tuple-element.37, bf16[2048,1536]{1,0:T(8,128)(2,1)} %get-tuple-element.36, f32[2048,576]{0,1:T(8,128)} %copy-done, f32[576]{0:T(1024)S(1)} %copy-done.35, f32[2048]{0:T(1024)S(1)} %copy-done.31), kind=kOutput, calls=%fused_computation.56 | convolution fusion | flops 7276462080 | bytes 24389888 | tf_op jit(solution)/shard_map/dot_general | solution.py:137
  623.8 4.5 copy.108
  628.3 5.7 fusion.32
  634.0 2.8 reshape.309
  636.8 18.1 %broadcast_multiply_fusion = f32[8,3,64,3,256]{4,2,3,1,0:T(8,128)} fusion(bf16[8,1024,3,64,1]{1,3,4,2,0:T(8,128)(2,1)S(1)} %bitcast.179, bf16[8,3,3,256,1024]{3,4,2,1,0:T(8,128)(2,1)} %fusion.2), kind=kOutput, calls=%fused_computation.65 | convolution fusion | flops 2417098752 | bytes 45613056 | tf_op jit(solution)/shard_map/shgqk,skhd->sqhgd/dot_general | solution.py:158
  654.9 5.2 copy_multiply_fusion
  663.1 2.7 copy.71
  668.1 2.7 add_convert_fusion.1
  670.8 2.8 copy.78
  673.6 6.2 fusion.22
  683.7 8.2 add_convert_fusion.2
  695.0 4.5 multiply_reduce_fusion.1
  699.5 4.3 add_convert_fusion
  705.4 41.2 %all-reduce.5 = f32[1152]{0:T(1024)S(1)} all-reduce(f32[1152]{0:T(1024)S(1)} %pad_maximum_fusion.14), channel_id=7, replica_groups=mesh['dp'=8,'ctx'=4] {'dp','ctx'}, use_global_device_ids=true, to_apply=%region_14.15.clone | all-reduce | flops 1152 | bytes 9216
  747.2 185.5 %all-reduce.9.cloned.1.call-done = (f32[552960]{0:T(1024)}, f32[331776]{0:T(1024)}, f32[1769472]{0:T(1024)}, f32[884736]{0:T(1024)}) async-done(((f32[552960]{0:T(1024)}, f32[331776]{0:T(1024)}, f32[1769472]{0:T(1024)}, f32[884736]{0:T(1024)}), (f32[552960]{0:T(1024)}, f32[331776]{0:T(1024)}, f32[1769472]{0:T(1024)}, f32[884736]{0:T(1024)})) %all-reduce.9.cloned.1.call-update) | async-done | bytes 14155792
  (165 shorter events, 65.2 us)
Async XLA Ops:
  7.2 63.9 %all-gather.13.cloned.1.call-start = ((), (), s32[]{:S(2)}) async-start(), calls=%async_computation.5 | async-start | bytes 2280960 | tf_op jit(solution)/shard_map/all_gather | solution.py:41
  8.7 152.6 %all-gather.11.cloned.1.call-start = ((), (), s32[]{:S(2)}) async-start(), calls=%async_computation.3 | async-start | bytes 1824768 | tf_op jit(solution)/shard_map/all_gather | solution.py:44
  9.4 182.1 %all-gather.9.cloned.1.call-start = ((), (), s32[]{:S(2)}) async-start(), calls=%async_computation.2 | async-start | bytes 3649536 | tf_op jit(solution)/shard_map/all_gather | solution.py:43
  10.2 229.4 %all-gather.7.cloned.1.call-start = ((), (), s32[]{:S(2)}) async-start(), calls=%async_computation.1 | async-start | bytes 7864320 | tf_op jit(solution)/shard_map/all_gather | solution.py:98
  53.8 2.8 copy-start.28
  59.9 99.2 %copy-start.22 = (f32[256,64]{0,1:T(8,128)}, f32[256,64]{0,1:T(8,128)S(1)}, u32[]{:S(2)}) copy-start(f32[256,64]{0,1:T(8,128)S(1)} %get-tuple-element.52) | copy-start | bytes 196612
  85.5 3.1 copy-start.7
  86.0 2.9 copy-start.24
  88.9 1.8 copy-start.33
  90.6 580.1 %reduce-scatter.2.cloned.1.call-start = ((), (), s32[]{:S(2)}) async-start(), calls=%async_computation.4 | async-start | bytes 7864320 | tf_op jit(solution)/shard_map/reduce_scatter | solution.py:177
  90.7 56.4 %copy-start.4 = (bf16[8,256,576]{1,2,0:T(8,128)(2,1)S(1)}, bf16[8,256,576]{1,2,0:T(8,128)(2,1)}, u32[]{:S(2)}) copy-start(bf16[8,256,576]{1,2,0:T(8,128)(2,1)} %param.7) | copy-start | bytes 7077892
  152.6 2.3 slice-start.4
  161.2 87.1 %copy-start.5 = (bf16[8,256,3,3,64]{1,4,3,2,0:T(8,128)(2,1)}, bf16[8,256,3,3,64]{1,4,3,2,0:T(8,128)(2,1)S(1)}, u32[]{:S(2)}) copy-start(bf16[8,256,3,3,64]{1,4,3,2,0:T(8,128)(2,1)S(1)} %fusion.18) | copy-start | bytes 7077892
  244.8 30.7 %copy-start.2 = (bf16[8,1024,192]{1,2,0:T(8,128)(2,1)}, bf16[8,1024,192]{1,2,0:T(8,128)(2,1)S(1)}, u32[]{:S(2)}) copy-start(bf16[8,1024,192]{1,2,0:T(8,128)(2,1)S(1)} %copy.60) | copy-start | bytes 9437188
  275.5 26.4 %copy-start.11 = (bf16[8,1024,192]{1,2,0:T(8,128)(2,1)S(1)}, bf16[8,1024,192]{1,2,0:T(8,128)(2,1)}, u32[]{:S(2)}) copy-start(bf16[8,1024,192]{1,2,0:T(8,128)(2,1)} %copy.59) | copy-start | bytes 9437188
  331.8 4.0 copy-start.16
  335.7 5.5 copy-start.9
  335.8 5.6 copy-start.15
  335.8 5.6 copy-start.34
  341.3 14.0 %copy-start = (f32[2048,576]{0,1:T(8,128)}, f32[2048,576]{0,1:T(8,128)S(1)}, u32[]{:S(2)}) copy-start(f32[2048,576]{0,1:T(8,128)S(1)} %get-tuple-element.60) | copy-start | bytes 14155780
  341.3 49.0 %copy-start.30 = (f32[2048]{0:T(1024)}, f32[2048]{0:T(1024)S(1)}, u32[]{:S(2)}) copy-start(f32[2048]{0:T(1024)S(1)} %add_rsqrt_fusion) | copy-start | bytes 24580
  376.8 13.5 %copy-start.1 = (f32[2048,576]{0,1:T(8,128)S(1)}, f32[2048,576]{0,1:T(8,128)}, u32[]{:S(2)}) copy-start(f32[2048,576]{0,1:T(8,128)} %copy-done) | copy-start | bytes 14155780
  376.8 13.5 %copy-start.12 = (bf16[8,72,8,256]{3,2,0,1:T(8,128)(2,1)S(1)}, bf16[8,72,8,256]{3,2,0,1:T(8,128)(2,1)}, u32[]{:S(2)}) copy-start(bf16[8,72,8,256]{3,2,0,1:T(8,128)(2,1)} %copy.96) | copy-start | bytes 7077892
  390.3 1.6 copy-start.17
  391.9 2.2 copy-start.8
  394.1 2.2 copy-start.26
  394.9 1.4 copy-start.14
  484.9 6.2 copy-start.27
  491.1 59.9 %copy-start.6 = (f32[1024,64]{0,1:T(8,128)S(1)}, f32[1024,64]{0,1:T(8,128)}, u32[]{:S(2)}) copy-start(f32[1024,64]{0,1:T(8,128)} %get-tuple-element.50) | copy-start | bytes 786436
  570.5 2.4 copy-start.21
  590.9 341.8 %all-reduce.9.cloned.1.call-start = ((), (), s32[]{:S(2)}) async-start(), calls=%async_computation.6 | async-start | bytes 28311552
  592.2 4.4 copy-start.13
  605.5 5.3 copy-start.31
  605.5 5.3 copy-start.35
  623.8 4.5 copy-start.10
  628.3 8.5 copy-start.3
  636.8 18.1 %copy-start.23 = (f32[256,64]{0,1:T(8,128)S(1)}, f32[256,64]{0,1:T(8,128)}, u32[]{:S(2)}) copy-start(f32[256,64]{0,1:T(8,128)} %copy-done.22) | copy-start | bytes 196612
  660.4 2.6 slice-start.2
  660.7 2.3 slice-start.3
  663.1 5.0 slice-start.5
  665.8 2.3 slice-start.6
  668.1 5.4 copy-start.29
  682.2 1.5 copy-start.19
  682.2 11.3 %slice-start = ((s8[4718592]{0:T(1024)(128)(4,1)}), s8[524288]{0:T(1024)(128)(4,1)S(1)}, s32[]{:S(2)}) async-start(s8[4718592]{0:T(1024)(128)(4,1)} %bitcast.168), calls=%async_computation.7 | async-start | bytes 1048576
  683.7 9.8 %slice-start.1 = ((s8[4718592]{0:T(1024)(128)(4,1)}), s8[4194304]{0:T(1024)(128)(4,1)S(1)}, s32[]{:S(2)}) async-start(s8[4718592]{0:T(1024)(128)(4,1)} %bitcast.168), calls=%async_computation.8 | async-start | bytes 8388608
  691.9 2.6 copy-start.18
  691.9 3.0 copy-start.20
  703.8 1.6 copy-start.36
  (2 other events, 1.6 us)
Sparse Core Ops, SparseCore 0:
  11.4 59.5 all-gather.12
  73.8 56.0 all-gather.10
  132.9 58.5 all-gather.8
  193.5 46.0 all-gather.6
  591.0 58.3 reduce-scatter.1
  682.3 250.3 all-reduce.8
where the time goes:
time: 955 us; the launch traced here: 946 us
  matrix products  291 us (30%)
  waiting for transfers between devices  265 us (28%)
  other arithmetic  143 us (15%)
  blocking collectives  129 us (14%)
  local copies, waits for them, and re-layouts  102 us (11%)
  between operations  15.1 us (2%)
    unnamed x7, waiting for transfers between devices  187 us
    unnamed x2, blocking collectives  83.3 us
    convert_element_type x1, other arithmetic, local(): grad_scores_low = (probs_again * (grad_probs - centre)).astype(jnp.bfloat16)  59.9 us
    dot_general x1, matrix products, local(): jnp.einsum('sqhgd,skhd->shgqk', grad_mixed_low, value_all, preferred_elem...  57.9 us
    all_gather x1, blocking collectives, fetch(): lax.all_gather(part_out, ('dp', 'ctx'), axis=0, tiled=True)  46.2 us
    all_gather x1, waiting for transfers between devices, local(): gathered = lax.all_gather(stacked, 'ctx', axis=1, tiled=True)  41.1 us
    unnamed x105, local copies, waits for them, and re-layouts  34.6 us
    dot_general x1, matrix products, local(): jnp.einsum('shgqk,sqhgd->skhd', prob_again_low, grad_mixed_low, preferred...  30.7 us
  transfers between devices with their start and end apart: 6, of which 4 were waited for; matrix products, arithmetic and copies ran while one was open for 17% of the time, Pallas kernels for 0%

commit v1 on v0

--- a/solution.py
+++ b/solution.py
@@ -95,7 +95,16 @@
         [key_low.reshape(seqs_here, span, kv_width), value_low.reshape(seqs_here, span, kv_width)],
         axis=-1,
     )
-    gathered = lax.all_gather(stacked, "ctx", axis=1, tiled=True)
+    buffers = [stacked]
+    cores_n = lax.axis_size("ctx")
+    for ix in tuple(range(cores_n - 1)):
+        t_next = lax.ppermute(buffers[-1], "ctx", [(q, (q + 1) % cores_n) for q in range(cores_n)])
+        buffers.append(t_next)
+    gathered = jnp.roll(
+        jnp.concatenate(buffers[::-1], axis=1),
+        (lax.axis_index("ctx") + 1) * stacked.shape[1],
+        axis=1,
+    )
     total_len = gathered.shape[1]
     key_all = gathered[..., :kv_width].reshape(seqs_here, total_len, KV_HEADS, HEAD)
     value_all = gathered[..., kv_width:].reshape(seqs_here, total_len, KV_HEADS, HEAD)

time: 955 us -> 940 us (0.984)
  waiting for transfers between devices: 265 us -> 237 us
    all_gather x1 -> x0, waiting for transfers between devices: 41.1 us -> none  [local(): gathered = lax.all_gather(stacked, 'ctx', axis=1, tiled=True)]
    ppermute x0 -> x3, waiting for transfers between devices: none -> 40.8 us  [local(): lax.ppermute(buffers[-1], 'ctx', [(q, (q + 1) % cores_n) for q in range(c...]
    all_gather x1, waiting for transfers between devices: 25.6 us -> 0.01 us  [fetch(): lax.all_gather(part_gu, ('dp', 'ctx'), axis=0, tiled=True)]
    unnamed x105 -> x123, local copies, waits for them, and re-layouts: 34.6 us -> 42.3 us
    unnamed x7 -> x6, waiting for transfers between devices: 187 us -> 186 us
  transfers between devices with their start and end apart: 6 -> 8, of which waited for: 4 -> 4; matrix products, arithmetic and copies ran while one was open for 17% -> 17% of each run, Pallas kernels for 0% -> 0%
where the time goes in v1:
time: 940 us; the launch traced here: 931 us
  matrix products  291 us (31%)
  waiting for transfers between devices  237 us (25%)
  other arithmetic  144 us (15%)
  blocking collectives  135 us (14%)
  local copies, waits for them, and re-layouts  108 us (11%)
  between operations  14.9 us (2%)
    unnamed x6, waiting for transfers between devices  186 us
    unnamed x2, blocking collectives  80.2 us
    convert_element_type x1, other arithmetic, local(): grad_scores_low = (probs_again * (grad_probs - centre)).astype(jnp.bfloat16)  59.9 us
    dot_general x1, matrix products, local(): jnp.einsum('sqhgd,skhd->shgqk', grad_mixed_low, value_all, preferred_elem...  57.8 us
    all_gather x1, blocking collectives, fetch(): lax.all_gather(part_out, ('dp', 'ctx'), axis=0, tiled=True)  55.2 us
    unnamed x123, local copies, waits for them, and re-layouts  42.3 us
    ppermute x3, waiting for transfers between devices, local(): lax.ppermute(buffers[-1], 'ctx', [(q, (q + 1) % cores_n) for q in range(c...  40.8 us
    dot_general x1, matrix products, local(): jnp.einsum('shgqk,sqhgd->skhd', prob_again_low, grad_mixed_low, preferred...  30.7 us
  transfers between devices with their start and end apart: 8, of which 4 were waited for; matrix products, arithmetic and copies ran while one was open for 17% of the time, Pallas kernels for 0%

profile of v1, /device:TPU:0, one launch (start us, length us, event | category | flops | bytes accessed | tf_op | source)
XLA Modules:
  0.0 931.0 jit_solution(6514824922681440657)
XLA Ops:
  11.1 42.0 %all-reduce = bf16[1152]{0:T(1024)(128)(2,1)S(1)} all-reduce(bf16[1152]{0:T(1024)(128)(2,1)S(1)} %dynamic-update-slice), channel_id=1, replica_groups=mesh['dp'=8,'ctx'=4] {'dp','ctx'}, use_global_device_ids=true, to_apply=%add | all-reduce | flops 1152 | bytes 4608
  59.9 11.1 %all-gather.10.cloned.1.call-done = bf16[32,1,17280]{2,1,0:T(2,128)(2,1)} async-done(((bf16[1,1,17280]{2,1,0:T(2,128)(2,1)}), bf16[32,1,17280]{2,1,0:T(2,128)(2,1)}) %all-gather.10.cloned.1.call-update) | async-done | bytes 1105936 | tf_op jit(solution)/shard_map/all_gather | solution.py:41
  71.0 7.7 reduce.1
  80.9 4.7 fusion.54
  89.8 20.4 %collective-permute-done = bf16[8,256,384]{1,0,2:T(8,128)(2,1)S(1)} collective-permute-done((bf16[8,256,384]{1,0,2:T(8,128)(2,1)S(1)}, bf16[8,256,384]{1,0,2:T(8,128)(2,1)S(1)}, u32[]{:S(2)}, u32[]{:S(2)}) %collective-permute-start) | collective-permute-done | bytes 1572896 | tf_op jit(solution)/shard_map/ppermute | solution.py:101
  110.2 2.7 convert_bitcast_fusion
  112.9 20.4 %collective-permute-done.1 = bf16[8,256,384]{1,0,2:T(8,128)(2,1)} collective-permute-done((bf16[8,256,384]{1,0,2:T(8,128)(2,1)S(1)}, bf16[8,256,384]{1,0,2:T(8,128)(2,1)}, u32[]{:S(2)}, u32[]{:S(2)}) %collective-permute-start.1) | collective-permute-done | bytes 1572896 | tf_op jit(solution)/shard_map/ppermute | solution.py:101
  133.3 55.2 %all-gather.1 = bf16[32,1,10368]{2,1,0:T(2,128)(2,1)S(1)} all-gather(bf16[1,1,10368]{2,1,0:T(2,128)(2,1)S(1)} %reshape.317), channel_id=1, replica_groups=mesh['dp'=8,'ctx'=4] {'dp','ctx'}, dimensions={0}, use_global_device_ids=true | all-gather | bytes 684288 | tf_op jit(solution)/shard_map/all_gather | solution.py:42
  188.5 4.0 reduce.2
  194.3 3.5 copy.96
  197.8 2.9 copy.94
  211.5 4.7 reshape.298
  216.2 6.9 reshape.297
  233.4 3.5 copy.59
  237.0 27.1 %fusion.9 = (f32[8,3,3,256]{3,2,1,0:T(4,128)S(1)}, f32[8,3,1024,256,3]{3,2,4,1,0:T(8,128)}) fusion(pred[256,1024]{0,1:T(8,128)(4,1)S(1)} %iota_compare_fusion, bf16[8,1024,3,64,1]{1,3,4,2,0:T(8,128)(2,1)S(1)} %bitcast.178, bf16[8,256,3,3,64]{1,4,3,2,0:T(8,128)(2,1)S(1)} %fusion.18), kind=kOutput, calls=%fused_computation.14 | convolution fusion | flops 2472523776 | bytes 81338368 | tf_op jit(solution)/shard_map/sqhgd,skhd->shgqk/dot_general | solution.py:62
  264.1 24.8 %fusion.3 = f32[8,3,3,256]{3,2,1,0:T(4,128)} fusion(f32[8,3,3,256]{3,2,1,0:T(4,128)S(1)} %get-tuple-element.57, f32[8,3,1024,256,3]{3,2,4,1,0:T(8,128)} %get-tuple-element.58, pred[256,1024]{0,1:T(8,128)(4,1)S(1)} %iota_compare_fusion), kind=kLoop, calls=%fused_computation.9 | loop fusion | flops 75479040 | bytes 75907072 | tf_op jit(solution)/shard_map/reduce_sum | solution.py:116
  290.5 29.8 %convert_bitcast_fusion.1 = bf16[8,256,3,3,64]{1,4,3,2,0:T(8,128)(2,1)} fusion(bf16[8,1024,3,64,1]{1,3,4,2,0:T(8,128)(2,1)S(1)} %bitcast.197, f32[8,3,3,256]{3,2,1,0:T(4,128)} %fusion.3, f32[8,3,3,256]{3,2,1,0:T(4,128)S(1)} %get-tuple-element.57, f32[8,3,1024,256,3]{3,2,4,1,0:T(8,128)} %get-tuple-element.58, pred[256,1024]{0,1:T(8,128)(4,1)S(1)} %iota_compare_fusion), kind=kOutput, calls=%fused_computation.67 | convolution fusion | flops 2511470592 | bytes 81412096 | tf_op jit(solution)/shard_map/shgqk,skhd->sqhgd/dot_general | solution.py:120
  320.3 3.2 copy.65
  324.4 5.5 multiply_reduce_fusion.4
  329.9 14.0 %fusion.51 = f32[2048,3072]{1,0:T(8,128)} fusion(bf16[576,3072]{1,0:T(8,128)(2,1)S(1)} %copy-done.20, f32[2048,576]{0,1:T(8,128)S(1)} %get-tuple-element.60, f32[576]{0:T(1024)S(1)} %copy-done.40, f32[2048]{0:T(1024)S(1)} %add_rsqrt_fusion), kind=kOutput, calls=%fused_computation.124 | convolution fusion | flops 7251296256 | bytes 33433856 | tf_op jit(solution)/shard_map/dot_general | solution.py:126
  343.9 21.5 %multiply_convert_fusion.1 = (bf16[2048,1536]{1,0:T(8,128)(2,1)}, bf16[2048,1536]{1,0:T(8,128)(2,1)}, bf16[2048,1536]{1,0:T(8,128)(2,1)}) fusion(f32[2048,3072]{1,0:T(8,128)} %fusion.51, bf16[2048,576]{0,1:T(8,128)(2,1)} %bitcast.200, bf16[1536,576]{1,0:T(8,128)(2,1)} %reshape.298), kind=kOutput, calls=%fused_computation.17 | convolution fusion | flops 3671064576 | bytes 48168960 | tf_op jit(solution)/shard_map/dot_general | solution.py:142
  365.4 13.5 %multiply_reduce_fusion = (f32[576]{0:T(1024)}, f32[2048]{0:T(1024)S(1)}, f32[2048,576]{0,1:T(8,128)S(1)}) fusion(f32[2048,576]{0,1:T(8,128)} %copy-done, f32[2048]{0:T(1024)S(1)} %add_rsqrt_fusion, f32[576]{0:T(1024)S(1)} %copy-done.40, bf16[576,3072]{1,0:T(8,128)(2,1)} %reshape.297, bf16[2048,1536]{1,0:T(8,128)(2,1)} %get-tuple-element.37, ...), kind=kOutput, calls=%fused_computation.41 | convolution fusion | flops 7279998464 | bytes 25580032 | tf_op jit(solution)/shard_map/dot_general | solution.py:147
  384.9 30.7 %bitcast_convert_fusion = bf16[8,3,64,1024]{3,2,1,0:T(8,128)(2,1)} fusion(f32[8,3,3,256]{3,2,1,0:T(4,128)S(1)} %copy-done.32, f32[8,3,1024,256,3]{3,2,4,1,0:T(8,128)} %get-tuple-element.58, pred[256,1024]{0,1:T(8,128)(4,1)S(1)} %iota_compare_fusion, bf16[8,256,3,3,64]{1,0,4,3,2:T(8,128)(2,1)S(1)} %bitcast.206), kind=kOutput, calls=%fused_computation.29 | convolution fusion | flops 2492989440 | bytes 81338368 | tf_op jit(solution)/shard_map/shgqk,sqhgd->skhd/dot_general | solution.py:173
  415.6 57.8 %fusion = (f32[8,3,3,256]{3,2,1,0:T(4,128)}, f32[8,3,1024,256,3]{3,2,4,1,0:T(8,128)}) fusion(f32[8,3,3,256]{3,2,1,0:T(4,128)S(1)} %copy-done.32, f32[8,3,1024,256,3]{3,2,4,1,0:T(8,128)} %get-tuple-element.58, pred[256,1024]{0,1:T(8,128)(4,1)S(1)} %iota_compare_fusion, bf16[8,1024,3,64,1]{1,3,4,2,0:T(8,128)(2,1)S(1)} %bitcast.198, ...), kind=kOutput, calls=%fused_computation.2 | convolution fusion | flops 2510272512 | bytes 156909568 | tf_op jit(solution)/shard_map/sqhgd,skhd->shgqk/dot_general | solution.py:162
  473.5 6.2 copy.77
  479.7 59.9 %fusion.2 = bf16[8,3,3,256,1024]{3,4,2,1,0:T(8,128)(2,1)} fusion(f32[8,3,1024,256,3]{3,2,4,1,0:T(8,128)} %get-tuple-element.63, f32[8,3,3,256]{3,2,1,0:T(4,128)S(1)} %copy-done.33, f32[8,3,3,256]{3,2,1,0:T(4,128)S(1)} %copy-done.32, f32[8,3,1024,256,3]{3,2,4,1,0:T(8,128)} %get-tuple-element.58, pred[256,1024]{0,1:T(8,128)(4,1)S(1)} %iota_compare_fusion), kind=kLoop, calls=%fused_computation.4 | loop fusion | flops 113246208 | bytes 189153280 | tf_op jit(solution)/shard_map/convert_element_type | solution.py:166
  539.6 19.4 %bitcast_multiply_fusion.1 = (f32[8,1024,3,64]{1,3,2,0:T(8,128)S(1)}, f32[8,3,64,1024,1]{3,2,4,1,0:T(8,128)}) fusion(f32[1024,64]{0,1:T(8,128)S(1)} %copy-done.6, bf16[8,256,3,3,64]{1,4,3,2,0:T(8,128)(2,1)} %copy-done.5, bf16[8,3,3,256,1024]{3,4,2,1,0:T(8,128)(2,1)} %fusion.2), kind=kOutput, calls=%fused_computation.30 | convolution fusion | flops 2417491968 | bytes 52953088 | tf_op jit(solution)/shard_map/shgqk,sqhgd->skhd/dot_general | solution.py:170
  561.5 5.5 fusion.13
  567.0 4.1 copy.76
  571.1 8.4 pad_maximum_fusion.3
  580.8 5.1 copy.106
  585.9 9.0 fusion.55
  594.9 5.4 reshape.311
  600.3 12.0 %fusion.19 = f32[72,24,8,128]{3,2,1,0:T(8,128)S(1)} fusion(bf16[2048,1536]{1,0:T(8,128)(2,1)} %get-tuple-element.37, bf16[2048,1536]{1,0:T(8,128)(2,1)} %get-tuple-element.36, f32[2048,576]{0,1:T(8,128)} %copy-done, f32[576]{0:T(1024)S(1)} %copy-done.41, f32[2048]{0:T(1024)S(1)} %copy-done.37), kind=kOutput, calls=%fused_computation.56 | convolution fusion | flops 7276462080 | bytes 24389888 | tf_op jit(solution)/shard_map/dot_general | solution.py:146
  612.4 4.4 copy.108
  616.8 5.7 fusion.32
  622.5 2.8 reshape.309
  625.4 18.2 %broadcast_multiply_fusion = f32[8,3,64,3,256]{4,2,3,1,0:T(8,128)} fusion(bf16[8,1024,3,64,1]{1,3,4,2,0:T(8,128)(2,1)S(1)} %bitcast.179, bf16[8,3,3,256,1024]{3,4,2,1,0:T(8,128)(2,1)} %fusion.2), kind=kOutput, calls=%fused_computation.65 | convolution fusion | flops 2417098752 | bytes 45613056 | tf_op jit(solution)/shard_map/shgqk,skhd->sqhgd/dot_general | solution.py:167
  643.6 5.2 copy_multiply_fusion
  651.7 2.7 copy.71
  656.8 2.7 add_convert_fusion.1
  659.4 2.8 copy.78
  662.2 6.2 fusion.22
  672.4 9.2 add_convert_fusion.2
  684.6 4.4 multiply_reduce_fusion.1
  689.0 4.4 add_convert_fusion
  695.0 38.2 %all-reduce.5 = f32[1152]{0:T(1024)S(1)} all-reduce(f32[1152]{0:T(1024)S(1)} %pad_maximum_fusion.14), channel_id=7, replica_groups=mesh['dp'=8,'ctx'=4] {'dp','ctx'}, use_global_device_ids=true, to_apply=%region_14.15.clone | all-reduce | flops 1152 | bytes 9216
  733.8 184.1 %all-reduce.9.cloned.1.call-done = (f32[552960]{0:T(1024)}, f32[331776]{0:T(1024)}, f32[1769472]{0:T(1024)}, f32[884736]{0:T(1024)}) async-done(((f32[552960]{0:T(1024)}, f32[331776]{0:T(1024)}, f32[1769472]{0:T(1024)}, f32[884736]{0:T(1024)}), (f32[552960]{0:T(1024)}, f32[331776]{0:T(1024)}, f32[1769472]{0:T(1024)}, f32[884736]{0:T(1024)})) %all-reduce.9.cloned.1.call-update) | async-done | bytes 14155792
  (188 shorter events, 72.1 us)
Async XLA Ops:
  7.2 63.9 %all-gather.10.cloned.1.call-start = ((), (), s32[]{:S(2)}) async-start(), calls=%async_computation.4 | async-start | bytes 2280960 | tf_op jit(solution)/shard_map/all_gather | solution.py:41
  8.7 202.8 %all-gather.8.cloned.1.call-start = ((), (), s32[]{:S(2)}) async-start(), calls=%async_computation.2 | async-start | bytes 1824768 | tf_op jit(solution)/shard_map/all_gather | solution.py:44
  9.4 206.8 %all-gather.6.cloned.1.call-start = ((), (), s32[]{:S(2)}) async-start(), calls=%async_computation.1 | async-start | bytes 3649536 | tf_op jit(solution)/shard_map/all_gather | solution.py:43
  10.2 649.3 %reduce-scatter.2.cloned.1.call-start = ((), (), s32[]{:S(2)}) async-start(), calls=%async_computation.3 | async-start | bytes 7864320 | tf_op jit(solution)/shard_map/reduce_scatter | solution.py:186
  53.8 5.3 copy-start.34
  59.9 149.4 %copy-start.27 = (f32[256,64]{0,1:T(8,128)}, f32[256,64]{0,1:T(8,128)S(1)}, u32[]{:S(2)}) copy-start(f32[256,64]{0,1:T(8,128)S(1)} %get-tuple-element.52) | copy-start | bytes 196612
  85.6 3.1 copy-start.8
  86.0 2.9 copy-start.29
  88.9 21.3 %copy-start.39 = (bf16[10368]{0:T(1024)(128)(2,1)S(1)}, bf16[10368]{0:T(1024)(128)(2,1)}, u32[]{:S(2)}) copy-start(bf16[10368]{0:T(1024)(128)(2,1)} %param.9) | copy-start | bytes 62212
  88.9 21.3 %copy-start.4 = (bf16[8,256,576]{1,2,0:T(8,128)(2,1)S(1)}, bf16[8,256,576]{1,2,0:T(8,128)(2,1)}, u32[]{:S(2)}) copy-start(bf16[8,256,576]{1,2,0:T(8,128)(2,1)} %param.7) | copy-start | bytes 7077892
  89.3 23.6 %copy-start.12 = (bf16[8,256,192]{1,0,2:T(8,128)(2,1)}, bf16[8,256,192]{1,0,2:T(8,128)(2,1)S(1)}, u32[]{:S(2)}) copy-start(bf16[8,256,192]{1,0,2:T(8,128)(2,1)S(1)} %fusion.31) | copy-start | bytes 2359300
  89.5 20.7 %collective-permute-start = (bf16[8,256,384]{1,0,2:T(8,128)(2,1)S(1)}, bf16[8,256,384]{1,0,2:T(8,128)(2,1)S(1)}, u32[]{:S(2)}, u32[]{:S(2)}) collective-permute-start(bf16[8,256,384]{1,0,2:T(8,128)(2,1)S(1)} %pad_maximum_fusion.11), channel_id=1, source_target_pairs={{0,1},{1,2},{2,3},{3,0},{4,5},{5,6},{6,7},{7,4},{8,9},{9,10},{10,1... | collective-permute-start | bytes 4718600 | tf_op jit(solution)/shard_map/ppermute | solution.py:101
  110.2 23.1 %copy-start.18 = (bf16[8,256,384]{1,0,2:T(8,128)(2,1)}, bf16[8,256,384]{1,0,2:T(8,128)(2,1)S(1)}, u32[]{:S(2)}) copy-start(bf16[8,256,384]{1,0,2:T(8,128)(2,1)S(1)} %collective-permute-done) | copy-start | bytes 4718596
  110.2 23.1 %collective-permute-start.1 = (bf16[8,256,384]{1,0,2:T(8,128)(2,1)S(1)}, bf16[8,256,384]{1,0,2:T(8,128)(2,1)}, u32[]{:S(2)}, u32[]{:S(2)}) collective-permute-start(bf16[8,256,384]{1,0,2:T(8,128)(2,1)S(1)} %collective-permute-done), channel_id=1, source_target_pairs={{0,1},{1,2},{2,3},{3,0},{4,5},{5,6},{6,7},{7,4},{8,9},{9,10},{10,1... | collective-permute-start | bytes 4718600 | tf_op jit(solution)/shard_map/ppermute | solution.py:101
  133.3 89.9 %collective-permute-start.2 = (bf16[8,256,384]{1,0,2:T(8,128)(2,1)}, bf16[8,256,384]{1,0,2:T(8,128)(2,1)}, u32[]{:S(2)}, u32[]{:S(2)}) collective-permute-start(bf16[8,256,384]{1,0,2:T(8,128)(2,1)} %collective-permute-done.1), channel_id=1, source_target_pairs={{0,1},{1,2},{2,3},{3,0},{4,5},{5,6},{6,7},{7,4},{8,9},{9,10},{10,1... | collective-permute-start | bytes 4718600 | tf_op jit(solution)/shard_map/ppermute | solution.py:101
  194.3 3.5 copy-start.7
  202.9 2.3 slice-start.4
  211.5 25.5 %copy-start.5 = (bf16[8,256,3,3,64]{1,4,3,2,0:T(8,128)(2,1)}, bf16[8,256,3,3,64]{1,4,3,2,0:T(8,128)(2,1)S(1)}, u32[]{:S(2)}) copy-start(bf16[8,256,3,3,64]{1,4,3,2,0:T(8,128)(2,1)S(1)} %fusion.18) | copy-start | bytes 7077892
  223.1 3.4 copy-start.19
  223.1 3.7 copy-start.13
  233.4 30.7 %copy-start.2 = (bf16[8,1024,192]{1,2,0:T(8,128)(2,1)}, bf16[8,1024,192]{1,2,0:T(8,128)(2,1)S(1)}, u32[]{:S(2)}) copy-start(bf16[8,1024,192]{1,2,0:T(8,128)(2,1)S(1)} %copy.60) | copy-start | bytes 9437188
  264.1 26.4 %copy-start.14 = (bf16[8,1024,192]{1,2,0:T(8,128)(2,1)S(1)}, bf16[8,1024,192]{1,2,0:T(8,128)(2,1)}, u32[]{:S(2)}) copy-start(bf16[8,1024,192]{1,2,0:T(8,128)(2,1)} %copy.59) | copy-start | bytes 9437188
  320.3 4.0 copy-start.21
  324.3 5.5 copy-start.10
  324.3 5.6 copy-start.20
  324.3 5.6 copy-start.40
  329.9 14.0 %copy-start = (f32[2048,576]{0,1:T(8,128)}, f32[2048,576]{0,1:T(8,128)S(1)}, u32[]{:S(2)}) copy-start(f32[2048,576]{0,1:T(8,128)S(1)} %get-tuple-element.60) | copy-start | bytes 14155780
  329.9 49.0 %copy-start.36 = (f32[2048]{0:T(1024)}, f32[2048]{0:T(1024)S(1)}, u32[]{:S(2)}) copy-start(f32[2048]{0:T(1024)S(1)} %add_rsqrt_fusion) | copy-start | bytes 24580
  365.4 13.5 %copy-start.1 = (f32[2048,576]{0,1:T(8,128)S(1)}, f32[2048,576]{0,1:T(8,128)}, u32[]{:S(2)}) copy-start(f32[2048,576]{0,1:T(8,128)} %copy-done) | copy-start | bytes 14155780
  365.4 13.5 %copy-start.15 = (bf16[8,72,8,256]{3,2,0,1:T(8,128)(2,1)S(1)}, bf16[8,72,8,256]{3,2,0,1:T(8,128)(2,1)}, u32[]{:S(2)}) copy-start(bf16[8,72,8,256]{3,2,0,1:T(8,128)(2,1)} %copy.96) | copy-start | bytes 7077892
  473.5 6.2 copy-start.33
  479.7 59.9 %copy-start.6 = (f32[1024,64]{0,1:T(8,128)S(1)}, f32[1024,64]{0,1:T(8,128)}, u32[]{:S(2)}) copy-start(f32[1024,64]{0,1:T(8,128)} %get-tuple-element.50) | copy-start | bytes 786436
  559.1 2.4 copy-start.26
  579.5 338.4 %all-reduce.9.cloned.1.call-start = ((), (), s32[]{:S(2)}) async-start(), calls=%async_computation.5 | async-start | bytes 28311552
  580.8 5.1 copy-start.16
  594.9 5.4 copy-start.37
  594.9 5.4 copy-start.41
  612.4 4.5 copy-start.11
  616.8 8.6 copy-start.3
  625.4 18.2 %copy-start.28 = (f32[256,64]{0,1:T(8,128)S(1)}, f32[256,64]{0,1:T(8,128)}, u32[]{:S(2)}) copy-start(f32[256,64]{0,1:T(8,128)} %copy-done.27) | copy-start | bytes 196612
  649.1 2.6 slice-start.2
  649.4 2.3 slice-start.3
  651.7 5.0 slice-start.5
  656.8 5.5 copy-start.35
  670.8 12.3 %slice-start = ((s8[4718592]{0:T(1024)(128)(4,1)}), s8[524288]{0:T(1024)(128)(4,1)S(1)}, s32[]{:S(2)}) async-start(s8[4718592]{0:T(1024)(128)(4,1)} %bitcast.168), calls=%async_computation.6 | async-start | bytes 1048576
  672.4 10.8 %slice-start.1 = ((s8[4718592]{0:T(1024)(128)(4,1)}), s8[4194304]{0:T(1024)(128)(4,1)S(1)}, s32[]{:S(2)}) async-start(s8[4718592]{0:T(1024)(128)(4,1)} %bitcast.168), calls=%async_computation.7 | async-start | bytes 8388608
  681.6 2.5 copy-start.23
  681.6 3.0 copy-start.25
  (10 other events, 15.9 us)
Sparse Core Ops, SparseCore 0:
  11.4 59.5 all-gather.9
  73.9 55.3 all-gather.7
  132.2 61.0 all-gather.5
  579.7 54.6 reduce-scatter.1
  671.0 246.9 all-reduce.8
